TPU v7x, 256 devices: a whole 4x4x8 slice. The times are simulated.
256 devices in a mesh: seg: 8 (over y, core), op: 32 (over z, x).
Axes of the slice: x: 4, y: 4, z: 8, core: 2. Of those that a mesh axis runs over, the one named last changes fastest.
Arguments:
- psi_start: bfloat16 [8, 32, 128, 128], P('seg', 'op'), may hold values from -4 to 4
- left_ops: bfloat16 [8, 128, 32, 128, 128], P('seg', 'op'), may hold values from -2 to 9, as said below
- right_ops: bfloat16 [8, 128, 32, 128, 128], P('seg', 'op'), may hold values from -2 to 9, as said below
- shifts: int32 [8, 128], P('seg', 'op'), may hold values from 0 to 31
- active: int32 [8, 128, 32], P('seg', 'op'), may hold values 0 or 1
Outputs:
- state: bfloat16 [8, 32, 128, 128], P('seg', 'op')
- rdm_pieces: float32 [8, 128], P('seg', 'op')
Inputs may be any that keep to these rules, and one draw needn't show every extreme that they name: `left_ops`: each block is a diagonal of entries between 1 and 7.8 plus off-diagonal entries of size about 2 / sqrt(128). `right_ops`: each block is a diagonal of entries between 1 and 7.8 plus off-diagonal entries of size about 2 / sqrt(128).
All inputs are finite; a program needn't handle non-finite values. No bound on the sum of `active` on one device may be relied on, other than what follows from the above.
Results may differ from a plain program's by a relative error of at most 0.0046.
Values may be sent and summed in bfloat16 or wider, within the bound.
A program may use at most 64 MiB of HBM per device.

v0:
```python
import jax
import jax.numpy as jnp
from jax import lax
from jax.sharding import PartitionSpec as P

ITERS = 3


precise = lax.Precision.HIGHEST
step_size = 0.3


def shifted(block, axis, distance):
    devices = range(lax.axis_size(axis))
    route = [(i - distance, i) for i in devices if i - distance in devices]
    return lax.ppermute(block, axis, route)


def blockmul(left, right):
    return jnp.einsum("sij,sjl->sil", left, right, precision=precise)


def neighbour_gram(piece):
    return jnp.einsum("sji,sjl->sil", piece, piece, preferred_element_type=jnp.float32)


def term_products(state_low, lefts, rights):
    half = jnp.einsum(
        "ksij,sjl->ksil", lefts, state_low, preferred_element_type=jnp.float32
    ).astype(jnp.bfloat16)
    return jnp.einsum("ksil,ksml->ksim", half, rights, preferred_element_type=jnp.float32)


def route_table(shift_row, weights, blocks_all):
    sources = lax.broadcasted_iota(jnp.int32, (shift_row.shape[0], blocks_all), 1)
    targets = (sources + shift_row[:, None]) % blocks_all
    places = lax.broadcasted_iota(jnp.int32, (shift_row.shape[0], blocks_all, blocks_all), 1)
    return (places == targets[:, None, :]).astype(jnp.float32) * weights[:, None, :]


def place_terms(table, products):
    return jnp.einsum("kts,ksim->tim", table, products, precision=precise)


def term_values(state_low, products, table, value_scale):
    cross = jnp.einsum("ksim,tim->kst", products, state_low.astype(jnp.float32), precision=precise)
    return jnp.einsum("kts,kst->k", table, cross, precision=precise) * value_scale


def shards(psi_start, left_ops, right_ops, shifts, active):
    lefts = left_ops[0]
    rights = right_ops[0]
    weights = active[0].astype(jnp.float32)
    shift_row = shifts[0]
    own_start = psi_start[0]
    blocks_dev = own_start.shape[0]
    width = own_start.shape[1]
    blocks_all = lefts.shape[1]
    term_scale = 1.0 / (lefts.shape[0] * lax.axis_size("op"))
    count = float(blocks_all * width * width)
    own_offset = lax.axis_index("op") * blocks_dev
    table = route_table(shift_row, weights, blocks_all)
    full_state = lax.all_gather(own_start, "op", axis=0, tiled=True).astype(jnp.float32)
    for sweep_index in range(ITERS):
        full_low = full_state.astype(jnp.bfloat16)
        products = term_products(full_low, lefts, rights)
        partial_terms = place_terms(table, products) * term_scale
        own_part = lax.dynamic_slice_in_dim(full_state, own_offset, blocks_dev, 0)
        env_own_low = own_part.astype(jnp.bfloat16)
        from_left = shifted(env_own_low, "seg", 1)
        from_right = shifted(env_own_low, "seg", -1)
        env = neighbour_gram(from_left) + neighbour_gram(from_right)
        placed = lax.dynamic_update_slice_in_dim(
            jnp.zeros_like(partial_terms), blockmul(own_part, env) * (0.5 / width), own_offset, 0
        )
        applied = lax.psum(partial_terms + placed, "op")
        rho = jnp.sum(full_state * applied) / jnp.sum(full_state * full_state)
        stepped = full_state - step_size * (applied - rho * full_state)
        full_state = stepped * jnp.sqrt(count / jnp.sum(stepped * stepped))
    full_low = full_state.astype(jnp.bfloat16)
    own_low = lax.dynamic_slice_in_dim(full_low, own_offset, blocks_dev, 0)
    final_products = term_products(full_low, lefts, rights)
    pieces = term_values(full_low, final_products, table, 1.0 / count)
    return (own_low[None], pieces[None])


def solution(mesh):
    return jax.shard_map(
        shards,
        mesh=mesh,
        in_specs=(
            P("seg", "op", None, None),
            P("seg", "op", None, None, None),
            P("seg", "op", None, None, None),
            P("seg", "op"),
            P("seg", "op", None),
        ),
        out_specs=(P("seg", "op", None, None), P("seg", "op")),
        check_vma=False,
    )
```

profile of v0, /device:TPU:8, one launch (start us, length us, event | category | flops | bytes accessed | tf_op | source)
XLA Modules:
  0.0 713.7 jit_solution(2968405341293279504)
XLA Ops:
  9.4 80.2 %all-gather.3.cloned.1.call-done = bf16[32,1,128,128]{3,2,1,0:T(8,128)(2,1)} async-done(((bf16[1,1,128,128]{3,2,1,0:T(8,128)(2,1)}), bf16[32,1,128,128]{3,2,1,0:T(8,128)(2,1)}) %all-gather.3.cloned.1.call-update) | async-done | bytes 1048592 | tf_op jit(solution)/shard_map/all_gather | solution.py:63
  93.3 2.4 collective-permute-start
  95.7 3.6 convert_bitcast_fusion.3
  99.3 3.1 fusion.17
  102.4 11.4 %fusion.36 = f32[32,128,128]{2,0,1:T(8,128)S(1)} fusion(f32[4,32,128,128]{3,2,1,0:T(8,128)S(1)} %fusion.17, f32[4,32]{1,0:T(4,128)S(1)} %convert_bitcast_fusion.4, s32[4,32]{1,0:T(4,128)S(1)} %add_select_fusion), kind=kOutput, calls=%fused_computation.45 | convolution fusion | flops 805314560 | bytes 10486784 | tf_op jit(solution)/shard_map/kts,ksim->tim/dot_general | solution.py:42
  120.2 152.7 %all-reduce.4.cloned.1.call-done = f32[32,128,128]{1,2,0:T(8,128)} async-done(((f32[32,128,128]{1,2,0:T(8,128)}), f32[32,128,128]{1,2,0:T(8,128)}) %all-reduce.4.cloned.1.call-update) | async-done | bytes 2097168 | tf_op jit(solution)/shard_map/psum | solution.py:76
  272.9 2.9 multiply_reduce_fusion.7
  279.1 2.2 fusion.63
  281.9 3.4 convert_bitcast_fusion.2
  285.3 2.0 collective-permute-start.3
  287.3 2.4 collective-permute-start.2
  289.8 5.3 fusion.12
  295.0 23.9 %fusion.39 = f32[32,128,128]{2,0,1:T(8,128)} fusion(f32[4,32,128,128]{3,2,1,0:T(8,128)S(1)} %fusion.12, f32[4,32]{1,0:T(4,128)S(1)} %convert_bitcast_fusion.4, s32[4,32]{1,0:T(4,128)S(1)} %add_select_fusion), kind=kOutput, calls=%fused_computation.46 | convolution fusion | flops 805314560 | bytes 10486784 | tf_op jit(solution)/shard_map/kts,ksim->tim/dot_general | solution.py:42
  318.9 3.0 copy.40
  321.9 3.1 broadcast_multiply_fusion.2
  327.2 151.8 %all-reduce.6.cloned.1.call-done = f32[32,128,128]{1,2,0:T(8,128)} async-done(((f32[32,128,128]{1,2,0:T(8,128)}), f32[32,128,128]{1,2,0:T(8,128)}) %all-reduce.6.cloned.1.call-update) | async-done | bytes 2097168 | tf_op jit(solution)/shard_map/psum | solution.py:76
  479.0 2.7 multiply_reduce_fusion.4
  483.1 2.7 multiply_reduce_fusion.3
  486.6 2.8 broadcast_multiply_fusion
  490.0 3.2 convert_bitcast_fusion.1
  495.1 2.4 collective-permute-start.4
  497.6 5.3 fusion.10
  502.9 12.6 %fusion.42 = f32[32,128,128]{2,0,1:T(8,128)} fusion(f32[4,32,128,128]{3,2,1,0:T(8,128)S(1)} %fusion.10, f32[4,32]{1,0:T(4,128)S(1)} %convert_bitcast_fusion.4, s32[4,32]{1,0:T(4,128)S(1)} %add_select_fusion), kind=kOutput, calls=%fused_computation.47 | convolution fusion | flops 805314560 | bytes 10486784 | tf_op jit(solution)/shard_map/kts,ksim->tim/dot_general | solution.py:42
  515.5 3.0 copy.47
  518.5 3.1 broadcast_multiply_fusion.1
  523.8 151.8 %all-reduce.8.cloned.1.call-done = f32[32,128,128]{1,2,0:T(8,128)} async-done(((f32[32,128,128]{1,2,0:T(8,128)}), f32[32,128,128]{1,2,0:T(8,128)}) %all-reduce.8.cloned.1.call-update) | async-done | bytes 2097168 | tf_op jit(solution)/shard_map/psum | solution.py:76
  675.6 2.7 multiply_reduce_fusion.1
  679.7 2.7 multiply_reduce_fusion
  683.2 2.2 multiply_convert_fusion
  686.0 3.2 convert_bitcast_fusion
  690.9 6.5 fusion.8
  697.4 8.9 %fusion.60 = f32[4]{0:T(128)S(1)} fusion(f32[4,32,32]{2,1,0:T(8,128)S(1)} %copy.75, f32[4,32,128,128]{3,2,1,0:T(8,128)S(1)} %fusion.8, bf16[32,128,128]{2,0,1:T(8,128)(2,1)S(1)} %copy.55), kind=kOutput, calls=%fused_computation.65 | convolution fusion | flops 805314560 | bytes 9453584 | tf_op jit(solution)/shard_map/ksim,tim->kst/dot_general | solution.py:46
  (60 shorter events, 23.6 us)
Async XLA Ops:
  7.2 82.4 %all-gather.3.cloned.1.call-start = ((), (), s32[]{:S(2)}) async-start(), calls=%async_computation.3 | async-start | bytes 1081344 | tf_op jit(solution)/shard_map/all_gather | solution.py:63
  7.9 265.0 %all-reduce.4.cloned.1.call-start = ((), (), s32[]{:S(2)}) async-start(), calls=%async_computation | async-start | bytes 4194304 | tf_op jit(solution)/shard_map/psum | solution.py:76
  89.6 6.1 copy-start.9
  91.3 26.2 %collective-permute-start.1 = (bf16[1,128,128]{1,2,0:T(8,128)(2,1)S(1)}, bf16[1,128,128]{1,2,0:T(8,128)(2,1)S(1)}, u32[]{:S(2)}, u32[]{:S(2)}) collective-permute-start(bf16[1,128,128]{1,2,0:T(8,128)(2,1)S(1)} %dynamic-slice_convert_fusion), channel_id=1, source_target_pairs={{32,0},{64,32},{96,64},{128,96},{160,128},{192,160},{224,192},{33,... | collective-permute-start | bytes 98312 | tf_op jit(solution)/shard_map/ppermute | solution.py:16
  93.3 24.4 %collective-permute-start = (bf16[1,128,128]{1,2,0:T(8,128)(2,1)S(1)}, bf16[1,128,128]{1,2,0:T(8,128)(2,1)S(1)}, u32[]{:S(2)}, u32[]{:S(2)}) collective-permute-start(bf16[1,128,128]{1,2,0:T(8,128)(2,1)S(1)} %dynamic-slice_convert_fusion), channel_id=1, source_target_pairs={{0,32},{32,64},{64,96},{96,128},{128,160},{160,192},{192,224},{1,3... | collective-permute-start | bytes 98312 | tf_op jit(solution)/shard_map/ppermute | solution.py:16
  95.7 3.7 copy-start.3
  118.9 1.3 copy-start.8
  120.2 358.9 %all-reduce.6.cloned.1.call-start = ((), (), s32[]{:S(2)}) async-start(), calls=%async_computation.1 | async-start | bytes 4194304 | tf_op jit(solution)/shard_map/psum | solution.py:76
  272.9 4.2 copy-start.7
  279.1 2.8 copy-start
  281.9 201.2 %copy-start.6 = (f32[32,128,128]{1,2,0:T(8,128)}, f32[32,128,128]{1,2,0:T(8,128)S(1)}, u32[]{:S(2)}) copy-start(f32[32,128,128]{1,2,0:T(8,128)S(1)} %fusion.63) | copy-start | bytes 6291460
  281.9 7.9 %copy-start.4 = (bf16[1,4,32,128,128]{4,3,2,1,0:T(8,128)(2,1)S(1)}, bf16[1,4,32,128,128]{4,3,2,1,0:T(8,128)(2,1)}, u32[]{:S(2)}) copy-start(bf16[1,4,32,128,128]{4,3,2,1,0:T(8,128)(2,1)} %param.7) | copy-start | bytes 12582916
  285.3 39.8 %collective-permute-start.3 = (bf16[1,128,128]{1,2,0:T(8,128)(2,1)S(1)}, bf16[1,128,128]{1,2,0:T(8,128)(2,1)S(1)}, u32[]{:S(2)}, u32[]{:S(2)}) collective-permute-start(bf16[1,128,128]{1,2,0:T(8,128)(2,1)S(1)} %dynamic-slice_convert_fusion.2), channel_id=1, source_target_pairs={{32,0},{64,32},{96,64},{128,96},{160,128},{192,160},{224,192},{33,... | collective-permute-start | bytes 98312 | tf_op jit(solution)/shard_map/ppermute | solution.py:16
  287.3 37.9 %collective-permute-start.2 = (bf16[1,128,128]{1,2,0:T(8,128)(2,1)S(1)}, bf16[1,128,128]{1,2,0:T(8,128)(2,1)S(1)}, u32[]{:S(2)}, u32[]{:S(2)}) collective-permute-start(bf16[1,128,128]{1,2,0:T(8,128)(2,1)S(1)} %dynamic-slice_convert_fusion.2), channel_id=1, source_target_pairs={{0,32},{32,64},{64,96},{96,128},{128,160},{160,192},{192,224},{1,3... | collective-permute-start | bytes 98312 | tf_op jit(solution)/shard_map/ppermute | solution.py:16
  327.1 348.4 %all-reduce.8.cloned.1.call-start = ((), (), s32[]{:S(2)}) async-start(), calls=%async_computation.2 | async-start | bytes 4194304 | tf_op jit(solution)/shard_map/psum | solution.py:76
  486.6 3.5 copy-start.1
  490.0 7.5 %copy-start.5 = (bf16[1,4,32,128,128]{4,3,2,1,0:T(8,128)(2,1)S(1)}, bf16[1,4,32,128,128]{4,3,2,1,0:T(8,128)(2,1)}, u32[]{:S(2)}) copy-start(bf16[1,4,32,128,128]{4,3,2,1,0:T(8,128)(2,1)} %param.7) | copy-start | bytes 12582916
  493.2 28.4 %collective-permute-start.5 = (bf16[1,128,128]{1,2,0:T(8,128)(2,1)S(1)}, bf16[1,128,128]{1,2,0:T(8,128)(2,1)S(1)}, u32[]{:S(2)}, u32[]{:S(2)}) collective-permute-start(bf16[1,128,128]{1,2,0:T(8,128)(2,1)S(1)} %dynamic-slice_convert_fusion.1), channel_id=1, source_target_pairs={{32,0},{64,32},{96,64},{128,96},{160,128},{192,160},{224,192},{33,... | collective-permute-start | bytes 98312 | tf_op jit(solution)/shard_map/ppermute | solution.py:16
  495.1 26.6 %collective-permute-start.4 = (bf16[1,128,128]{1,2,0:T(8,128)(2,1)S(1)}, bf16[1,128,128]{1,2,0:T(8,128)(2,1)S(1)}, u32[]{:S(2)}, u32[]{:S(2)}) collective-permute-start(bf16[1,128,128]{1,2,0:T(8,128)(2,1)S(1)} %dynamic-slice_convert_fusion.1), channel_id=1, source_target_pairs={{0,32},{32,64},{64,96},{96,128},{128,160},{160,192},{192,224},{1,3... | collective-permute-start | bytes 98312 | tf_op jit(solution)/shard_map/ppermute | solution.py:16
  683.1 2.8 copy-start.2
Sparse Core Ops, SparseCore 0:
  10.6 78.9 all-gather.2
  120.3 152.5 all-reduce.3
  327.3 151.7 all-reduce.5
  523.9 151.6 all-reduce.7
where the time goes:
time: 723 us; the launch traced here: 714 us
  waiting for transfers between devices  537 us (74%)
  matrix products  95.8 us (13%)
  other arithmetic  32.1 us (4%)
  between operations  20.6 us (3%)
  local copies, waits for them, and re-layouts  14.7 us (2%)
  starting transfers between devices  13.2 us (2%)
    psum x3, waiting for transfers between devices, shards(): applied = lax.psum(partial_terms + placed, 'op')  456 us
    all_gather x1, waiting for transfers between devices, shards(): lax.all_gather(own_start, 'op', axis=0, tiled=True).astype(jnp.float32)  80.2 us
    dot_general x3, matrix products, place_terms(): return jnp.einsum('kts,ksim->tim', table, products, precision=precise)  47.9 us
    dot_general x4, matrix products, term_products(): jnp.einsum('ksil,ksml->ksim', half, rights, preferred_element_type=jnp.fl...  20.2 us
  transfers between devices with their start and end apart: 10, of which 4 were waited for; matrix products, arithmetic and copies ran while one was open for 12% of the time, Pallas kernels for 0%

commit v1 on v0

v1 whole, which is shorter than its diff:
```python
import functools

import jax
import jax.numpy as jnp
from jax import lax
from jax.experimental import pallas as pl
from jax.experimental.pallas import tpu as pltpu
from jax.sharding import PartitionSpec as P

ITERS = 3
STEP = 0.3
MESH = pl.DeviceIdType.MESH
F32 = jnp.float32
BF16 = jnp.bfloat16


def kernel(
    nz, nx, nseg, axis_terms,
    psi_ref, left_hbm, right_hbm, shift_ref, active_ref,
    state_ref, rdm_ref,
    left_v, right_v, half_v, ag, xsend, xrecv, own_acc, zsend, zrecv,
    scz, scx, nbr, cur_v, tcur_v, app_v,
    load_sem, ag_zs, ag_zr, ag_xs, ag_xr, rs_xs, rs_xr, rs_zs, rs_zr,
    sc_zs, sc_zr, sc_xs, sc_xr, nb_s, nb_r,
):
    terms, blocks, width = left_v.shape[0], left_v.shape[1], left_v.shape[2]
    count = float(blocks * width * width)
    term_scale = 1.0 / (terms * axis_terms)
    seg = lax.axis_index("seg")
    me = lax.axis_index("op")
    z, x = me // nx, me % nx

    def device(zz, xx):
        return (seg, zz * nx + xx)

    def remote(src, dst, send_sem, recv_sem, where):
        return pltpu.make_async_remote_copy(
            src_ref=src, dst_ref=dst, send_sem=send_sem, recv_sem=recv_sem,
            device_id=where, device_id_type=MESH,
        )

    def near_first(i):
        hop = i // 2 + 1
        return hop + (i % 2) * (nz - 2 * hop)

    left_load = pltpu.make_async_copy(left_hbm, left_v, load_sem.at[0])
    right_load = pltpu.make_async_copy(right_hbm, right_v, load_sem.at[1])
    left_load.start()
    right_load.start()

    seg_up = (seg + 1) % nseg
    seg_down = (seg + nseg - 1) % nseg
    barrier = pltpu.get_barrier_semaphore()
    for dz in range(1, nz):
        pl.semaphore_signal(barrier, inc=1, device_id=device((z + dz) % nz, x), device_id_type=MESH)
    for dx in range(1, nx):
        pl.semaphore_signal(barrier, inc=1, device_id=device(z, (x + dx) % nx), device_id_type=MESH)
    for other in (seg_up, seg_down):
        pl.semaphore_signal(barrier, inc=1, device_id=(other, me), device_id_type=MESH)
    pl.semaphore_wait(barrier, nz - 1 + nx - 1 + 2)

    def gather_z(p, dz):
        return remote(ag.at[p, z, x], ag.at[p, z, x], ag_zs.at[p, dz], ag_zr.at[p, dz],
                      device((z + dz) % nz, x))

    def gather_z_in(p, dz):
        block = ag.at[p, (z + nz - dz) % nz, x]
        return remote(block, block, ag_zs.at[p, dz], ag_zr.at[p, dz], device((z + dz) % nz, x))

    def gather_x(p, dz, dx):
        block = ag.at[p, (z + nz - dz) % nz, x]
        return remote(block, block, ag_xs.at[p, dz, dx], ag_xr.at[p, dz, dx], device(z, (x + dx) % nx))

    def gather_x_in(p, dz, dx):
        block = ag.at[p, (z + nz - dz) % nz, (x + nx - dx) % nx]
        return remote(block, block, ag_xs.at[p, dz, dx], ag_xr.at[p, dz, dx], device(z, (x + dx) % nx))

    def gather_start(p):
        for i in reversed(range(nz - 1)):
            gather_z(p, near_first(i)).start()
        for dx in range(1, nx):
            gather_x(p, 0, dx).start()

    def half_block(p, bz, bx):
        s = bz * nx + bx
        stacked = left_v[:, s].reshape(terms * width, width)
        half = jnp.dot(stacked, ag[p, bz, bx], preferred_element_type=F32)
        for k in range(terms):
            weight = active_ref[k, s].astype(F32)
            half_v[k, s] = (half[k * width:(k + 1) * width] * weight).astype(BF16)

    def gather_column(p):
        def arrive(i, carry):
            dz = near_first(i)
            gather_z_in(p, dz).wait_recv()
            for dx in range(1, nx):
                gather_x(p, dz, dx).start()
            half_block(p, (z + nz - dz) % nz, x)
            return carry
        half_block(p, z, x)
        lax.fori_loop(0, nz - 1, arrive, 0)

    def gather_rest(p):
        def row(i, carry):
            dz = i
            for dx in range(1, nx):
                gather_x_in(p, dz, dx).wait_recv()
                half_block(p, (z + nz - dz) % nz, (x + nx - dx) % nx)
            return carry
        lax.fori_loop(0, nz, row, 0)

    def gathered(t):
        halves, rights = [], []
        for k in range(terms):
            s = lax.rem(t + blocks - shift_ref[k], blocks)
            halves.append(half_v[k, s])
            rights.append(right_v[k, s])
        return jnp.concatenate(halves, axis=1), jnp.concatenate(rights, axis=1)

    def term_block(t):
        halves, rights = gathered(t)
        return lax.dot_general(halves, rights, (((1,), (1,)), ((), ())), preferred_element_type=F32)

    def scatter_x(q, dz, dx):
        return remote(xsend.at[q, dz, dx - 1], xrecv.at[q, dz, dx - 1], rs_xs.at[q, dz, dx],
                      rs_xr.at[q, dz, dx], device(z, (x + dx) % nx))

    def scatter_z(q, dz):
        return remote(zsend.at[q, dz], zrecv.at[q, dz], rs_zs.at[q, dz], rs_zr.at[q, dz],
                      device((z + dz) % nz, x))

    def scatter_send(q):
        def row(i, carry):
            dz = nz - 1 - i
            base = ((z + dz) % nz) * nx
            for dx in range(1, nx):
                xsend[q, dz, dx - 1] = term_block(base + (x + dx) % nx).astype(BF16)
                scatter_x(q, dz, dx).start()
            own_acc[dz] = term_block(base + x)
            return carry
        lax.fori_loop(0, nz, row, 0)

    def column_sum(q, dz):
        total = own_acc[dz]
        for dx in range(1, nx):
            scatter_x(q, dz, dx).wait_recv()
            total = total + xrecv[q, dz, dx - 1].astype(F32)
        return total

    def scatter_finish(q):
        def row(i, carry):
            dz = nz - 1 - i
            zsend[q, dz] = column_sum(q, dz).astype(BF16)
            scatter_z(q, dz).start()
            return carry
        lax.fori_loop(0, nz - 1, row, 0)
        total = column_sum(q, 0)
        for dz in range(1, nz):
            scatter_z(q, dz).wait_recv()
            total = total + zrecv[q, dz].astype(F32)
        return total * term_scale

    def scalars_z(q, dz):
        return remote(scz.at[q, z], scz.at[q, z], sc_zs.at[q, dz], sc_zr.at[q, dz],
                      device((z + dz) % nz, x))

    def scalars_x(q, dx):
        return remote(scx.at[q, x], scx.at[q, x], sc_xs.at[q, dx], sc_xr.at[q, dx],
                      device(z, (x + dx) % nx))

    def scalars_start(q, cur, applied):
        rows = lax.broadcasted_iota(jnp.int32, (8, width), 0)
        a = jnp.sum(cur * applied)
        b = jnp.sum(cur * cur)
        c = jnp.sum(applied * applied)
        scz[q, z] = jnp.where(rows == 0, a, jnp.where(rows == 1, b, c))
        for dz in range(1, nz):
            scalars_z(q, dz).start()

    def scalars_middle(q):
        for dz in range(1, nz):
            scalars_z(q, dz).wait_recv()
        total = scz[q, 0]
        for zz in range(1, nz):
            total = total + scz[q, zz]
        scx[q, x] = total
        for dx in range(1, nx):
            scalars_x(q, dx).start()

    def scalars_end(q):
        for dx in range(1, nx):
            scalars_x(q, dx).wait_recv()
        total = scx[q, 0]
        for xx in range(1, nx):
            total = total + scx[q, xx]
        a, b, c = total[0:1], total[1:2], total[2:3]
        rho = a / b
        norm = b + (STEP * STEP) * jnp.maximum(c - a * rho, 0.0)
        scale = jnp.sqrt(count / norm)
        return scale * (1.0 + STEP * rho), scale * STEP

    def neighbours(n):
        up = remote(nbr.at[n, 2], nbr.at[n, 0], nb_s.at[n, 0], nb_r.at[n, 0], (seg_up, me))
        down = remote(nbr.at[n, 2], nbr.at[n, 1], nb_s.at[n, 1], nb_r.at[n, 1], (seg_down, me))
        return up, down

    def neighbours_start(n, low):
        nbr[n, 2] = low
        for copy in neighbours(n):
            copy.start()

    has_left = (seg > 0).astype(F32)
    has_right = (seg < nseg - 1).astype(F32)

    def environment(n, cur):
        for copy in neighbours(n):
            copy.wait_recv()
        first = (nbr[n, 0].astype(F32) * has_left).astype(BF16)
        second = (nbr[n, 1].astype(F32) * has_right).astype(BF16)
        both = jnp.concatenate([first, second], axis=0)
        env = lax.dot_general(both, both, (((0,), (0,)), ((), ())), preferred_element_type=F32)
        return jnp.dot(cur, env, precision=lax.Precision.HIGHEST, preferred_element_type=F32) * (0.5 / width)

    start = psi_ref[0, 0]
    ag[0, z, x] = start
    gather_start(0)
    neighbours_start(0, start)
    cur_v[...] = start.astype(F32)
    left_load.wait()
    right_load.wait()

    for n in range(ITERS):
        gather_column(n)
        if n > 0:
            scalars_middle(n - 1)
        gather_rest(n)
        if n > 0:
            keep, take = scalars_end(n - 1)
            cur_v[...] = keep * cur_v[...] - take * app_v[...]
            neighbours_start(n, cur_v[...].astype(BF16))
        scatter_send(n)
        env_part = environment(n, cur_v[...])
        total = scatter_finish(n)
        if n > 0:
            total = keep * tcur_v[...] - take * total
        tcur_v[...] = total
        applied = total + env_part
        app_v[...] = applied
        if n < ITERS - 1:
            ag[n + 1, z, x] = applied.astype(BF16)
            gather_start(n + 1)
        scalars_start(n, cur_v[...], applied)

    scalars_middle(ITERS - 1)
    keep, take = scalars_end(ITERS - 1)
    final = (keep * cur_v[...] - take * app_v[...]).astype(BF16)
    ag[ITERS, z, x] = final
    gather_start(ITERS)
    state_ref[0, 0] = final
    gather_column(ITERS)
    gather_rest(ITERS)

    def values(t, acc):
        halves, rights = gathered(t)
        crossed = jnp.dot(ag[ITERS, t // nx, t % nx], rights, preferred_element_type=F32)
        crossed = crossed * halves.astype(F32)
        return acc + jnp.sum(crossed.reshape(width // 8, 8, terms * width), axis=0)

    acc = lax.fori_loop(0, blocks, values, jnp.zeros((8, terms * width), F32))
    for k in range(terms):
        rdm_ref[0, k] = jnp.sum(acc[:, k * width:(k + 1) * width]) * (1.0 / count)

    def drain_gather(p, carry):
        for dz in range(1, nz):
            gather_z(p, dz).wait_send()
        for dz in range(nz):
            for dx in range(1, nx):
                gather_x(p, dz, dx).wait_send()
        return carry

    lax.fori_loop(0, ITERS + 1, drain_gather, 0)

    def drain_iter(n, carry):
        for dz in range(nz):
            for dx in range(1, nx):
                scatter_x(n, dz, dx).wait_send()
        for dz in range(1, nz):
            scatter_z(n, dz).wait_send()
            scalars_z(n, dz).wait_send()
        for dx in range(1, nx):
            scalars_x(n, dx).wait_send()
        for copy in neighbours(n):
            copy.wait_send()
        return carry

    lax.fori_loop(0, ITERS, drain_iter, 0)


def shards(nseg, nop, psi_start, left_ops, right_ops, shifts, active):
    nx = 4 if nop == 32 else 2
    nz = nop // nx
    terms, blocks, width = left_ops.shape[1], left_ops.shape[2], left_ops.shape[3]
    vmem, dma = pltpu.VMEM, pltpu.SemaphoreType.DMA
    tile = (width, width)
    return pl.pallas_call(
        functools.partial(kernel, nz, nx, nseg, nop),
        out_shape=(
            jax.ShapeDtypeStruct((1, 1) + tile, BF16),
            jax.ShapeDtypeStruct((1, terms), F32),
        ),
        in_specs=[
            pl.BlockSpec(memory_space=pltpu.VMEM),
            pl.BlockSpec(memory_space=pl.ANY),
            pl.BlockSpec(memory_space=pl.ANY),
            pl.BlockSpec(memory_space=pltpu.SMEM),
            pl.BlockSpec(memory_space=pltpu.SMEM),
        ],
        out_specs=(
            pl.BlockSpec(memory_space=pltpu.VMEM),
            pl.BlockSpec(memory_space=pltpu.SMEM),
        ),
        scratch_shapes=[
            vmem((terms, blocks) + tile, BF16),
            vmem((terms, blocks) + tile, BF16),
            vmem((terms, blocks) + tile, BF16),
            vmem((ITERS + 1, nz, nx) + tile, BF16),
            vmem((ITERS, nz, nx - 1) + tile, BF16),
            vmem((ITERS, nz, nx - 1) + tile, BF16),
            vmem((nz,) + tile, F32),
            vmem((ITERS, nz) + tile, BF16),
            vmem((ITERS, nz) + tile, BF16),
            vmem((ITERS, nz, 8, width), F32),
            vmem((ITERS, nx, 8, width), F32),
            vmem((ITERS, 3) + tile, BF16),
            vmem(tile, F32),
            vmem(tile, F32),
            vmem(tile, F32),
            dma((2,)),
            dma((ITERS + 1, nz)),
            dma((ITERS + 1, nz)),
            dma((ITERS + 1, nz, nx)),
            dma((ITERS + 1, nz, nx)),
            dma((ITERS, nz, nx)),
            dma((ITERS, nz, nx)),
            dma((ITERS, nz)),
            dma((ITERS, nz)),
            dma((ITERS, nz)),
            dma((ITERS, nz)),
            dma((ITERS, nx)),
            dma((ITERS, nx)),
            dma((ITERS, 2)),
            dma((ITERS, 2)),
        ],
        compiler_params=pltpu.CompilerParams(
            collective_id=0, has_side_effects=True, vmem_limit_bytes=48 * 1024 * 1024
        ),
        name="chain",
    )(
        psi_start,
        left_ops.reshape(left_ops.shape[1:]),
        right_ops.reshape(right_ops.shape[1:]),
        shifts.reshape(terms),
        active.reshape(terms, blocks),
    )


def solution(mesh):
    return jax.shard_map(
        functools.partial(shards, mesh.shape["seg"], mesh.shape["op"]),
        mesh=mesh,
        in_specs=(
            P("seg", "op", None, None),
            P("seg", "op", None, None, None),
            P("seg", "op", None, None, None),
            P("seg", "op"),
            P("seg", "op", None),
        ),
        out_specs=(P("seg", "op", None, None), P("seg", "op")),
        check_vma=False,
    )
```

time: 723 us -> 159 us (0.22); the launches traced: 714 us -> 158 us
  waiting for transfers between devices: 537 us -> 0 us
  Pallas kernels: 0 us -> 152 us
  matrix products: 95.8 us -> 0 us
  other arithmetic: 32.1 us -> 0 us
  between operations: 20.6 us -> 0.65 us
  starting transfers between devices: 13.2 us -> 0 us
  local copies, waits for them, and re-layouts: 14.7 us -> 5.4 us
    psum x3 -> x0, waiting for transfers between devices: 456 us -> none  [shards(): applied = lax.psum(partial_terms + placed, 'op')]
    pallas_call x0 -> x1, Pallas kernels: none -> 152 us  [shards(): pl.pallas_call(functools.partial(kernel, nz, nx, nseg, nop), out_shape=(j...]
    dot_general x21 -> x0, matrix products: 95.8 us -> none  [the longest x3 47.9 us: place_terms(): return jnp.einsum('kts,ksim->tim', table, products, precision=precise)]
    all_gather x1 -> x0, waiting for transfers between devices: 80.2 us -> none  [shards(): lax.all_gather(own_start, 'op', axis=0, tiled=True).astype(jnp.float32)]
    reduce_sum x6 -> x0, other arithmetic: 15 us -> none  [the longest x3 8.36 us: shards(): rho = jnp.sum(full_state * applied) / jnp.sum(full_state * full_state)]
    ppermute x6 -> x0, starting transfers between devices: 13.1 us -> none  [shifted(): return lax.ppermute(block, axis, route)]
    mul x5 -> x0, other arithmetic: 12.9 us -> none  [the longest x3 7.98 us: shards(): partial_terms = place_terms(table, products) * term_scale]
    dot_general x3 -> x0, local copies, waits for them, and re-layouts: 7.98 us -> none  [place_terms(): return jnp.einsum('kts,ksim->tim', table, products, precision=precise)]
  transfers between devices with their start and end apart: 10 -> 0, of which waited for: 4 -> 0; matrix products, arithmetic and copies ran while one was open for 12% -> 0% of each run, Pallas kernels for 0% -> 0%
where the time goes in v1:
time: 159 us; the launch traced here: 158 us
  Pallas kernels  152 us (96%)
  local copies, waits for them, and re-layouts  5.4 us (3%)
    pallas_call x1, Pallas kernels, shards(): pl.pallas_call(functools.partial(kernel, nz, nx, nseg, nop), out_shape=(j...  152 us
    unnamed x10, local copies, waits for them, and re-layouts  5.4 us

profile of v1, /device:TPU:8, one launch (start us, length us, event | category | flops | bytes accessed | tf_op | source)
XLA Modules:
  0.0 158.1 jit_solution(5928152045577661462)
XLA Ops:
  0.6 0.0 copy-start
  0.6 2.2 %copy-done = bf16[1,4,32,128,128]{4,3,2,1,0:T(8,128)(2,1)S(1)} copy-done((bf16[1,4,32,128,128]{4,3,2,1,0:T(8,128)(2,1)S(1)}, bf16[1,4,32,128,128]{4,3,2,1,0:T(8,128)(2,1)}, u32[]{:S(2)}) %copy-start) | copy-done | bytes 4194328
  2.8 0.0 copy-start.1
  2.8 0.8 copy-done.1
  3.6 0.0 copy-start.2
  3.6 0.7 copy-done.2
  4.3 0.0 copy-start.3
  4.3 0.7 copy-done.3
  4.9 152.1 %chain.1 = (bf16[1,1,128,128]{3,2,1,0:T(8,128)(2,1)S(1)}, f32[1,4]{1,0:T(1,128)S(1)}) custom-call(bf16[1,1,128,128]{3,2,1,0:T(8,128)(2,1)S(1)} %copy-done.1, bf16[4,32,128,128]{3,2,1,0:T(8,128)(2,1)S(1)} %bitcast.4, bf16[4,32,128,128]{3,2,1,0:T(8,128)(2,1)} %bitcast.7, s32[4]{0:T(128)S(1)} %bitcast.6, s32[4,32]{1,0:T(4,128)S(1)} %bitcast.5), custom_call_target="tpu_custom_call" | custom-call | tf_op jit(solution)/shard_map/chain/pallas_call | solution.py:305
  157.0 0.6 copy.9
  157.6 0.5 copy.10
Async XLA Ops:
  0.6 2.2 %copy-start = (bf16[1,4,32,128,128]{4,3,2,1,0:T(8,128)(2,1)S(1)}, bf16[1,4,32,128,128]{4,3,2,1,0:T(8,128)(2,1)}, u32[]{:S(2)}) copy-start(bf16[1,4,32,128,128]{4,3,2,1,0:T(8,128)(2,1)} %param.6) | copy-start | bytes 12582916
  2.8 0.8 copy-start.1
  3.6 0.7 copy-start.2
  4.3 0.7 copy-start.3

commit v2 on v1

v2 whole, which is shorter than its diff:
```python
import functools

import jax
import jax.numpy as jnp
from jax import lax
from jax.experimental import pallas as pl
from jax.experimental.pallas import tpu as pltpu
from jax.sharding import PartitionSpec as P

ITERS = 3
STEP = 0.3
MESH = pl.DeviceIdType.MESH
F32 = jnp.float32
BF16 = jnp.bfloat16


def kernel(
    nz, nx, nseg, axis_terms,
    psi_hbm, left_hbm, right_hbm, shift_ref, active_ref,
    state_ref, rdm_ref,
    psi_v, left_v, right_v, half_v, ag, xsend, xrecv, own_acc, zsend, zrecv,
    scz, scx, nbr, cur_v, tcur_v, app_v,
    load_sem, ag_zs, ag_zr, ag_xs, ag_xr, rs_xs, rs_xr, rs_zs, rs_zr,
    sc_zs, sc_zr, sc_xs, sc_xr, nb_s, nb_r,
):
    terms, blocks, width = left_v.shape[0], left_v.shape[1], left_v.shape[2]
    count = float(blocks * width * width)
    term_scale = 1.0 / (terms * axis_terms)
    others = nx - 1
    seg = lax.axis_index("seg")
    me = lax.axis_index("op")
    z, x = me // nx, me % nx
    x_order = (1, 3, 2) if nx == 4 else (1,)

    def device(dz, dx):
        return (seg, ((z + dz) % nz) * nx + (x + dx) % nx)

    def slot(dz, dx):
        return ((z + nz - dz) % nz) * nx + (x + nx - dx) % nx

    def remote(src, dst, send_sem, recv_sem, where):
        return pltpu.make_async_remote_copy(
            src_ref=src, dst_ref=dst, send_sem=send_sem, recv_sem=recv_sem,
            device_id=where, device_id_type=MESH,
        )

    def near_first(i):
        hop = (i + 1) // 2
        return (hop + ((i + 1) % 2) * (nz - 2 * hop)) % nz

    psi_load = pltpu.make_async_copy(psi_hbm.at[0, 0], psi_v, load_sem.at[0])
    left_load = pltpu.make_async_copy(left_hbm, left_v, load_sem.at[1])
    right_load = pltpu.make_async_copy(right_hbm, right_v, load_sem.at[2])
    psi_load.start()
    left_load.start()
    right_load.start()

    seg_up = (seg + 1) % nseg
    seg_down = (seg + nseg - 1) % nseg
    barrier = pltpu.get_barrier_semaphore()
    for dz in range(1, nz):
        pl.semaphore_signal(barrier, inc=1, device_id=device(dz, 0), device_id_type=MESH)
    for dx in range(1, nx):
        pl.semaphore_signal(barrier, inc=1, device_id=device(0, dx), device_id_type=MESH)
    for other in (seg_up, seg_down):
        pl.semaphore_signal(barrier, inc=1, device_id=(other, me), device_id_type=MESH)
    psi_load.wait()
    start = psi_v[...]
    ag[0, me] = start
    nbr[0, 2] = start
    cur_v[...] = start.astype(F32)
    pl.semaphore_wait(barrier, nz - 1 + nx - 1 + 2)

    def gather_z(p, dz):
        return remote(ag.at[p, me], ag.at[p, me], ag_zs.at[p], ag_zr.at[p, dz], device(dz, 0))

    def gather_x(p, dz, dx):
        block = ag.at[p, slot(dz, 0)]
        return remote(block, block, ag_xs.at[p], ag_xr.at[p, dz], device(0, dx))

    def gather_start(p):
        for i in range(1, nz):
            gather_z(p, near_first(i)).start()
            if i == min(2, nz - 1):
                for dx in x_order:
                    gather_x(p, 0, dx).start()

    def half_row(p, dz):
        stacked = []
        for dx in range(nx):
            s = slot(dz, dx)
            ops = left_v[:, s].reshape(terms * width, width)
            stacked.append((s, jnp.dot(ops, ag[p, s], preferred_element_type=F32)))
        for s, half in stacked:
            for k in range(terms):
                weight = active_ref[k, s].astype(F32)
                half_v[k, s] = (half[k * width:(k + 1) * width] * weight).astype(BF16)

    def gather_column(p):
        def arrive(i, carry):
            dz = near_first(i)
            block = ag.at[p, slot(dz, 0)]
            remote(block, block, ag_zs.at[p], ag_zr.at[p, dz], device(dz, 0)).wait_recv()
            for dx in x_order:
                gather_x(p, dz, dx).start()
            return carry
        lax.fori_loop(1, nz, arrive, 0)

    def gather_rest(p):
        def row(i, carry):
            dz = near_first(i)
            three = ag.at[p, pl.ds(0, others)]
            remote(three, three, ag_xs.at[p], ag_xr.at[p, dz], device(0, 1)).wait_recv()
            half_row(p, dz)
            return carry
        lax.fori_loop(0, nz, row, 0)

    def gathered(t):
        halves, rights = [], []
        for k in range(terms):
            s = lax.rem(t + blocks - shift_ref[k], blocks)
            halves.append(half_v[k, s])
            rights.append(right_v[k, s])
        return jnp.concatenate(halves, axis=1), jnp.concatenate(rights, axis=1)

    def term_block(t):
        halves, rights = gathered(t)
        return lax.dot_general(halves, rights, (((1,), (1,)), ((), ())), preferred_element_type=F32)

    def scatter_x(q, dz, dx):
        place = dz * others + dx - 1
        return remote(xsend.at[q, place], xrecv.at[q, place], rs_xs.at[q], rs_xr.at[q, dz], device(0, dx))

    def scatter_z(q, dz):
        return remote(zsend.at[q, dz - 1], zrecv.at[q, dz - 1], rs_zs.at[q], rs_zr.at[q], device(dz, 0))

    def scatter_send(q):
        def row(i, carry):
            dz = near_first(nz - 1 - i)
            base = ((z + dz) % nz) * nx
            parts = [term_block(base + (x + dx) % nx) for dx in range(nx)]
            own_acc[dz] = parts[0]
            for dx in x_order:
                xsend[q, dz * others + dx - 1] = parts[dx].astype(BF16)
            for dx in x_order:
                scatter_x(q, dz, dx).start()
            return carry
        lax.fori_loop(0, nz, row, 0)

    def column_sum(q, dz):
        three = pl.ds(dz * others, others)
        remote(xsend.at[q, three], xrecv.at[q, three], rs_xs.at[q], rs_xr.at[q, dz], device(0, 1)).wait_recv()
        total = own_acc[dz]
        for dx in range(1, nx):
            total = total + xrecv[q, dz * others + dx - 1].astype(F32)
        return total

    def scatter_finish(q):
        def row(i, carry):
            dz = near_first(nz - 1 - i)
            zsend[q, dz - 1] = column_sum(q, dz).astype(BF16)
            scatter_z(q, dz).start()
            return carry
        lax.fori_loop(0, nz - 1, row, 0)
        total = column_sum(q, 0)
        remote(zsend.at[q], zrecv.at[q], rs_zs.at[q], rs_zr.at[q], device(1, 0)).wait_recv()
        for dz in range(1, nz):
            total = total + zrecv[q, dz - 1].astype(F32)
        return total * term_scale

    def scalars_z(q, dz):
        return remote(scz.at[q, z], scz.at[q, z], sc_zs.at[q], sc_zr.at[q], device(dz, 0))

    def scalars_x(q, dx):
        return remote(scx.at[q, x], scx.at[q, x], sc_xs.at[q], sc_xr.at[q], device(0, dx))

    def scalars_start(q, cur, applied):
        rows = lax.broadcasted_iota(jnp.int32, (8, width), 0)
        a = jnp.sum(cur * applied)
        b = jnp.sum(cur * cur)
        c = jnp.sum(applied * applied)
        scz[q, z] = jnp.where(rows == 0, a, jnp.where(rows == 1, b, c))
        for i in range(1, nz):
            scalars_z(q, near_first(nz - i)).start()

    def scalars_middle(q):
        many = scz.at[q, pl.ds(0, nz - 1)]
        remote(many, many, sc_zs.at[q], sc_zr.at[q], device(1, 0)).wait_recv()
        total = scz[q, 0]
        for zz in range(1, nz):
            total = total + scz[q, zz]
        scx[q, x] = total
        for dx in range(1, nx):
            scalars_x(q, dx).start()

    def scalars_end(q):
        many = scx.at[q, pl.ds(0, others)]
        remote(many, many, sc_xs.at[q], sc_xr.at[q], device(0, 1)).wait_recv()
        total = scx[q, 0]
        for xx in range(1, nx):
            total = total + scx[q, xx]
        a, b, c = total[0:1], total[1:2], total[2:3]
        rho = a / b
        norm = b + (STEP * STEP) * jnp.maximum(c - a * rho, 0.0)
        scale = jnp.sqrt(count / norm)
        return scale * (1.0 + STEP * rho), scale * STEP

    def neighbours(n):
        up = remote(nbr.at[n, 2], nbr.at[n, 0], nb_s.at[n, 0], nb_r.at[n, 0], (seg_up, me))
        down = remote(nbr.at[n, 2], nbr.at[n, 1], nb_s.at[n, 1], nb_r.at[n, 1], (seg_down, me))
        return up, down

    has_left = (seg > 0).astype(F32)
    has_right = (seg < nseg - 1).astype(F32)

    def environment(n, cur):
        for copy in neighbours(n):
            copy.wait_recv()
        first = (nbr[n, 0].astype(F32) * has_left).astype(BF16)
        second = (nbr[n, 1].astype(F32) * has_right).astype(BF16)
        both = jnp.concatenate([first, second], axis=0)
        env = lax.dot_general(both, both, (((0,), (0,)), ((), ())), preferred_element_type=F32)
        return jnp.dot(cur, env, precision=lax.Precision.HIGHEST, preferred_element_type=F32) * (0.5 / width)

    gather_start(0)
    for copy in neighbours(0):
        copy.start()

    for n in range(ITERS):
        gather_column(n)
        if n == 0:
            left_load.wait()
            right_load.wait()
        else:
            scalars_middle(n - 1)
        gather_rest(n)
        scatter_send(n)
        if n > 0:
            keep, take = scalars_end(n - 1)
            cur = keep * cur_v[...] - take * app_v[...]
            cur_v[...] = cur
            nbr[n, 2] = cur.astype(BF16)
            for copy in neighbours(n):
                copy.start()
            tcur_v[...] = keep * tcur_v[...]
        app_v[...] = environment(n, cur_v[...])
        total = scatter_finish(n)
        if n > 0:
            total = tcur_v[...] - take * total
        applied = total + app_v[...]
        if n < ITERS - 1:
            ag[n + 1, me] = applied.astype(BF16)
            gather_start(n + 1)
        tcur_v[...] = total
        app_v[...] = applied
        scalars_start(n, cur_v[...], applied)

    scalars_middle(ITERS - 1)
    keep, take = scalars_end(ITERS - 1)
    final = (keep * cur_v[...] - take * app_v[...]).astype(BF16)
    ag[ITERS, me] = final
    gather_start(ITERS)
    state_ref[0, 0] = final
    gather_column(ITERS)
    gather_rest(ITERS)

    def values(t, acc):
        halves, rights = gathered(t)
        crossed = jnp.dot(ag[ITERS, t], rights, preferred_element_type=F32)
        crossed = crossed * halves.astype(F32)
        return acc + jnp.sum(crossed.reshape(width // 8, 8, terms * width), axis=0)

    acc = lax.fori_loop(0, blocks, values, jnp.zeros((8, terms * width), F32), unroll=4)
    for k in range(terms):
        rdm_ref[0, k] = jnp.sum(acc[:, k * width:(k + 1) * width]) * (1.0 / count)

    for p in range(ITERS + 1):
        column = ag.at[p, pl.ds(0, nz - 1)]
        rest = ag.at[p, pl.ds(0, nz * others)]
        remote(column, column, ag_zs.at[p], ag_zr.at[p, 0], device(1, 0)).wait_send()
        remote(rest, rest, ag_xs.at[p], ag_xr.at[p, 0], device(0, 1)).wait_send()
    for n in range(ITERS):
        remote(xsend.at[n], xrecv.at[n], rs_xs.at[n], rs_xr.at[n, 0], device(0, 1)).wait_send()
        remote(zsend.at[n], zrecv.at[n], rs_zs.at[n], rs_zr.at[n], device(1, 0)).wait_send()
        many = scz.at[n, pl.ds(0, nz - 1)]
        remote(many, many, sc_zs.at[n], sc_zr.at[n], device(1, 0)).wait_send()
        many = scx.at[n, pl.ds(0, others)]
        remote(many, many, sc_xs.at[n], sc_xr.at[n], device(0, 1)).wait_send()
        for copy in neighbours(n):
            copy.wait_send()


def shards(nseg, nop, psi_start, left_ops, right_ops, shifts, active):
    nx = 4 if nop == 32 else 2
    nz = nop // nx
    terms, blocks, width = left_ops.shape[1], left_ops.shape[2], left_ops.shape[3]
    vmem, dma = pltpu.VMEM, pltpu.SemaphoreType.DMA
    tile = (width, width)
    return pl.pallas_call(
        functools.partial(kernel, nz, nx, nseg, nop),
        out_shape=(
            jax.ShapeDtypeStruct((1, 1) + tile, BF16),
            jax.ShapeDtypeStruct((1, terms), F32),
        ),
        in_specs=[
            pl.BlockSpec(memory_space=pltpu.HBM),
            pl.BlockSpec(memory_space=pltpu.HBM),
            pl.BlockSpec(memory_space=pltpu.HBM),
            pl.BlockSpec(memory_space=pltpu.SMEM),
            pl.BlockSpec(memory_space=pltpu.SMEM),
        ],
        out_specs=(
            pl.BlockSpec(memory_space=pltpu.VMEM),
            pl.BlockSpec(memory_space=pltpu.SMEM),
        ),
        scratch_shapes=[
            vmem(tile, BF16),
            vmem((terms, blocks) + tile, BF16),
            vmem((terms, blocks) + tile, BF16),
            vmem((terms, blocks) + tile, BF16),
            vmem((ITERS + 1, nop) + tile, BF16),
            vmem((ITERS, nz * (nx - 1)) + tile, BF16),
            vmem((ITERS, nz * (nx - 1)) + tile, BF16),
            vmem((nz,) + tile, F32),
            vmem((ITERS, nz - 1) + tile, BF16),
            vmem((ITERS, nz - 1) + tile, BF16),
            vmem((ITERS, nz, 8, width), F32),
            vmem((ITERS, nx, 8, width), F32),
            vmem((ITERS, 3) + tile, BF16),
            vmem(tile, F32),
            vmem(tile, F32),
            vmem(tile, F32),
            dma((3,)),
            dma((ITERS + 1,)),
            dma((ITERS + 1, nz)),
            dma((ITERS + 1,)),
            dma((ITERS + 1, nz)),
            dma((ITERS,)),
            dma((ITERS, nz)),
            dma((ITERS,)),
            dma((ITERS,)),
            dma((ITERS,)),
            dma((ITERS,)),
            dma((ITERS,)),
            dma((ITERS,)),
            dma((ITERS, 2)),
            dma((ITERS, 2)),
        ],
        compiler_params=pltpu.CompilerParams(
            collective_id=0, has_side_effects=True, vmem_limit_bytes=63 * 1024 * 1024
        ),
        name="chain",
    )(
        psi_start,
        left_ops.reshape(left_ops.shape[1:]),
        right_ops.reshape(right_ops.shape[1:]),
        shifts.reshape(terms),
        active.reshape(terms, blocks),
    )


def solution(mesh):
    return jax.shard_map(
        functools.partial(shards, mesh.shape["seg"], mesh.shape["op"]),
        mesh=mesh,
        in_specs=(
            P("seg", "op", None, None),
            P("seg", "op", None, None, None),
            P("seg", "op", None, None, None),
            P("seg", "op"),
            P("seg", "op", None),
        ),
        out_specs=(P("seg", "op", None, None), P("seg", "op")),
        check_vma=False,
    )
```

time: 159 us -> 129 us (0.81)
  Pallas kernels: 152 us -> 125 us
  local copies, waits for them, and re-layouts: 5.4 us -> 2.55 us
    pallas_call x1, Pallas kernels: 152 us -> 125 us  [shards(): pl.pallas_call(functools.partial(kernel, nz, nx, nseg, nop), out_shape=(j...]
    unnamed x10 -> x2, local copies, waits for them, and re-layouts: 5.4 us -> 2.55 us
where the time goes in v2:
time: 129 us
  Pallas kernels  125 us (97%)
  local copies, waits for them, and re-layouts  2.55 us (2%)
    pallas_call x1, Pallas kernels, shards(): pl.pallas_call(functools.partial(kernel, nz, nx, nseg, nop), out_shape=(j...  125 us

profile of v2, /device:TPU:8, one launch (start us, length us, event | category | flops | bytes accessed | tf_op | source)
XLA Modules:
  0.0 128.6 jit_solution(6139792915447577476)
XLA Ops:
  0.6 125.4 %chain.1 = (bf16[1,1,128,128]{3,2,1,0:T(8,128)(2,1)}, f32[1,4]{1,0:T(1,128)}) custom-call(bf16[1,1,128,128]{3,2,1,0:T(8,128)(2,1)} %psi_hbm.1, bf16[4,32,128,128]{3,2,1,0:T(8,128)(2,1)} %bitcast.4, bf16[4,32,128,128]{3,2,1,0:T(8,128)(2,1)} %bitcast.5, s32[4]{0:T(128)} %bitcast.7, s32[4,32]{1,0:T(4,128)} %bitcast.6), custom_call_target="tpu_custom_call" | custom-call | tf_op jit(solution)/shard_map/chain/pallas_call | solution.py:299
  126.0 1.4 %copy.9 = bf16[1,1,128,128]{3,2,1,0:T(8,128)(2,1)} copy(bf16[1,1,128,128]{3,2,1,0:T(8,128)(2,1)} %get-tuple-element.4) | data formatting | bytes 65536
  127.4 1.2 copy.10

commit v3 on v2

--- a/solution.py
+++ b/solution.py
@@ -14,13 +14,44 @@
 BF16 = jnp.bfloat16
 
 
+TREE = (
+    ((1, 0), (0, 0)), ((7, 0), (0, 0)), ((0, 1), (0, 0)), ((0, 3), (0, 0)),
+    ((0, 2), (0, 0)), ((2, 0), (0, 0)), ((6, 0), (0, 0)), ((1, 1), (1, 0)),
+    ((1, 3), (1, 0)), ((2, 1), (1, 0)), ((1, 2), (0, 2)), ((7, 2), (7, 0)),
+    ((2, 3), (2, 0)), ((4, 0), (7, 0)), ((6, 1), (6, 0)), ((6, 3), (6, 0)),
+    ((5, 3), (6, 0)), ((3, 2), (0, 2)), ((2, 2), (2, 1)), ((7, 1), (1, 1)),
+    ((3, 1), (2, 1)), ((7, 3), (7, 2)), ((4, 3), (4, 0)), ((3, 0), (4, 0)),
+    ((3, 3), (2, 3)), ((4, 1), (4, 0)), ((6, 2), (6, 3)), ((5, 1), (6, 1)),
+    ((5, 0), (5, 3)), ((4, 2), (3, 2)), ((5, 2), (5, 3)),
+)
+
+
+def gather_tree(nz, nx):
+    if (nz, nx) == (8, 4):
+        tree = TREE
+    else:
+        tree = tuple(((dz, 0), (0, 0)) for dz in range(1, nz))
+        tree += tuple(((dz, dx), (dz, 0)) for dz in range(nz) for dx in range(1, nx))
+    kids = {}
+    for child, parent in tree:
+        kids.setdefault(parent, []).append(child)
+
+    def hops(child, parent):
+        up, right = (child[0] - parent[0]) % nz, (child[1] - parent[1]) % nx
+        return min(up, nz - up) + min(right, nx - right)
+
+    for parent, children in kids.items():
+        children.sort(key=lambda child: (hops(child, parent), -len(kids.get(child, ()))))
+    return [child for child, _ in tree], kids
+
+
 def kernel(
     nz, nx, nseg, axis_terms,
-    psi_hbm, left_hbm, right_hbm, shift_ref, active_ref,
-    state_ref, rdm_ref,
-    psi_v, left_v, right_v, half_v, ag, xsend, xrecv, own_acc, zsend, zrecv,
+    psi_hbm, left_hbm, right_hbm, shift_hbm, active_hbm,
+    state_hbm, rdm_ref,
+    psi_v, shift_ref, active_ref, left_v, right_v, half_v, ag, xsend, xrecv, own_acc, zsend, zrecv,
     scz, scx, nbr, cur_v, tcur_v, app_v,
-    load_sem, ag_zs, ag_zr, ag_xs, ag_xr, rs_xs, rs_xr, rs_zs, rs_zr,
+    load_sem, ag_s, ag_r, rs_xs, rs_xr, rs_zs, rs_zr,
     sc_zs, sc_zr, sc_xs, sc_xr, nb_s, nb_r,
 ):
     terms, blocks, width = left_v.shape[0], left_v.shape[1], left_v.shape[2]
@@ -52,16 +83,22 @@
     left_load = pltpu.make_async_copy(left_hbm, left_v, load_sem.at[1])
     right_load = pltpu.make_async_copy(right_hbm, right_v, load_sem.at[2])
     psi_load.start()
+    shift_load = pltpu.make_async_copy(shift_hbm, shift_ref, load_sem.at[3])
+    active_load = pltpu.make_async_copy(active_hbm, active_ref, load_sem.at[4])
     left_load.start()
     right_load.start()
+    shift_load.start()
+    active_load.start()
 
     seg_up = (seg + 1) % nseg
     seg_down = (seg + nseg - 1) % nseg
+    order, kids = gather_tree(nz, nx)
+    steps = {((c[0] - p[0]) % nz, (c[1] - p[1]) % nx) for p in kids for c in kids[p]}
+    steps |= {(dz, 0) for dz in range(1, nz)} | {(0, dx) for dx in range(1, nx)}
+    steps |= {((nz - dz) % nz, (nx - dx) % nx) for dz, dx in steps}
     barrier = pltpu.get_barrier_semaphore()
-    for dz in range(1, nz):
-        pl.semaphore_signal(barrier, inc=1, device_id=device(dz, 0), device_id_type=MESH)
-    for dx in range(1, nx):
-        pl.semaphore_signal(barrier, inc=1, device_id=device(0, dx), device_id_type=MESH)
+    for dz, dx in sorted(steps):
+        pl.semaphore_signal(barrier, inc=1, device_id=device(dz, dx), device_id_type=MESH)
     for other in (seg_up, seg_down):
         pl.semaphore_signal(barrier, inc=1, device_id=(other, me), device_id_type=MESH)
     psi_load.wait()
@@ -69,56 +106,52 @@
     ag[0, me] = start
     nbr[0, 2] = start
     cur_v[...] = start.astype(F32)
-    pl.semaphore_wait(barrier, nz - 1 + nx - 1 + 2)
-
-    def gather_z(p, dz):
-        return remote(ag.at[p, me], ag.at[p, me], ag_zs.at[p], ag_zr.at[p, dz], device(dz, 0))
-
-    def gather_x(p, dz, dx):
-        block = ag.at[p, slot(dz, 0)]
-        return remote(block, block, ag_xs.at[p], ag_xr.at[p, dz], device(0, dx))
-
-    def gather_start(p):
-        for i in range(1, nz):
-            gather_z(p, near_first(i)).start()
-            if i == min(2, nz - 1):
-                for dx in x_order:
-                    gather_x(p, 0, dx).start()
-
-    def half_row(p, dz):
+    pl.semaphore_wait(barrier, len(steps) + 2)
+
+    def arrival(p, offset):
+        block = ag.at[p, slot(*offset)]
+        place = offset[0] * nx + offset[1]
+        return remote(block, block, ag_s.at[p], ag_r.at[p, place], device(1, 0))
+
+    def forward(p, parent):
+        block = ag.at[p, slot(*parent)]
+        for child in kids.get(parent, ()):
+            place = child[0] * nx + child[1]
+            where = device((child[0] - parent[0]) % nz, (child[1] - parent[1]) % nx)
+            remote(block, block, ag_s.at[p], ag_r.at[p, place], where).start()
+
+    def half_blocks(p, offsets):
         stacked = []
-        for dx in range(nx):
-            s = slot(dz, dx)
+        for offset in offsets:
+            s = slot(*offset)
             ops = left_v[:, s].reshape(terms * width, width)
             stacked.append((s, jnp.dot(ops, ag[p, s], preferred_element_type=F32)))
         for s, half in stacked:
             for k in range(terms):
-                weight = active_ref[k, s].astype(F32)
+                weight = active_ref[0, k, s].astype(F32)
                 half_v[k, s] = (half[k * width:(k + 1) * width] * weight).astype(BF16)
 
-    def gather_column(p):
-        def arrive(i, carry):
-            dz = near_first(i)
-            block = ag.at[p, slot(dz, 0)]
-            remote(block, block, ag_zs.at[p], ag_zr.at[p, dz], device(dz, 0)).wait_recv()
-            for dx in x_order:
-                gather_x(p, dz, dx).start()
-            return carry
-        lax.fori_loop(1, nz, arrive, 0)
-
-    def gather_rest(p):
-        def row(i, carry):
-            dz = near_first(i)
-            three = ag.at[p, pl.ds(0, others)]
-            remote(three, three, ag_xs.at[p], ag_xr.at[p, dz], device(0, 1)).wait_recv()
-            half_row(p, dz)
-            return carry
-        lax.fori_loop(0, nz, row, 0)
+    busy = [i for i, offset in enumerate(order) if offset in kids]
+    pauses = (4, 8)
+
+    def gather(p, midway=None):
+        ready = [(0, 0)]
+        for i, offset in enumerate(order):
+            arrival(p, offset).wait_recv()
+            forward(p, offset)
+            ready.append(offset)
+            while len(ready) >= 4 and (i >= busy[-1] or i in pauses):
+                half_blocks(p, ready[:4])
+                ready = ready[4:]
+            if midway is not None and i == pauses[-1]:
+                midway()
+        if ready:
+            half_blocks(p, ready)
 
     def gathered(t):
         halves, rights = [], []
         for k in range(terms):
-            s = lax.rem(t + blocks - shift_ref[k], blocks)
+            s = lax.rem(t + blocks - shift_ref[0, k], blocks)
             halves.append(half_v[k, s])
             rights.append(right_v[k, s])
         return jnp.concatenate(halves, axis=1), jnp.concatenate(rights, axis=1)
@@ -155,17 +188,27 @@
             total = total + xrecv[q, dz * others + dx - 1].astype(F32)
         return total
 
+    def encode(ref, block):
+        largest = jnp.maximum(jnp.max(jnp.abs(block), keepdims=True), 1e-30)
+        exponent = jnp.ceil(jnp.log2(largest)) - 14.0
+        ref[:width] = jnp.floor(block * jnp.exp2(-exponent) + 0.5).astype(jnp.int32).astype(jnp.int16)
+        ref[width:] = jnp.broadcast_to(exponent, (16, width)).astype(jnp.int32).astype(jnp.int16)
+
+    def decode(ref):
+        exponent = ref[width:].astype(jnp.int32).astype(F32)[0:1]
+        return ref[:width].astype(jnp.int32).astype(F32) * jnp.exp2(exponent)
+
     def scatter_finish(q):
         def row(i, carry):
             dz = near_first(nz - 1 - i)
-            zsend[q, dz - 1] = column_sum(q, dz).astype(BF16)
+            encode(zsend.at[q, dz - 1], column_sum(q, dz))
             scatter_z(q, dz).start()
             return carry
         lax.fori_loop(0, nz - 1, row, 0)
         total = column_sum(q, 0)
         remote(zsend.at[q], zrecv.at[q], rs_zs.at[q], rs_zr.at[q], device(1, 0)).wait_recv()
         for dz in range(1, nz):
-            total = total + zrecv[q, dz - 1].astype(F32)
+            total = total + decode(zrecv.at[q, dz - 1])
         return total * term_scale
 
     def scalars_z(q, dz):
@@ -222,18 +265,17 @@
         env = lax.dot_general(both, both, (((0,), (0,)), ((), ())), preferred_element_type=F32)
         return jnp.dot(cur, env, precision=lax.Precision.HIGHEST, preferred_element_type=F32) * (0.5 / width)
 
-    gather_start(0)
+    forward(0, (0, 0))
     for copy in neighbours(0):
         copy.start()
 
     for n in range(ITERS):
-        gather_column(n)
         if n == 0:
             left_load.wait()
             right_load.wait()
-        else:
-            scalars_middle(n - 1)
-        gather_rest(n)
+            shift_load.wait()
+            active_load.wait()
+        gather(n, functools.partial(scalars_middle, n - 1) if n > 0 else None)
         scatter_send(n)
         if n > 0:
             keep, take = scalars_end(n - 1)
@@ -250,7 +292,7 @@
         applied = total + app_v[...]
         if n < ITERS - 1:
             ag[n + 1, me] = applied.astype(BF16)
-            gather_start(n + 1)
+            forward(n + 1, (0, 0))
         tcur_v[...] = total
         app_v[...] = applied
         scalars_start(n, cur_v[...], applied)
@@ -259,10 +301,10 @@
     keep, take = scalars_end(ITERS - 1)
     final = (keep * cur_v[...] - take * app_v[...]).astype(BF16)
     ag[ITERS, me] = final
-    gather_start(ITERS)
-    state_ref[0, 0] = final
-    gather_column(ITERS)
-    gather_rest(ITERS)
+    forward(ITERS, (0, 0))
+    state_store = pltpu.make_async_copy(ag.at[ITERS, me], state_hbm.at[0, 0], load_sem.at[5])
+    state_store.start()
+    gather(ITERS)
 
     def values(t, acc):
         halves, rights = gathered(t)
@@ -274,11 +316,10 @@
     for k in range(terms):
         rdm_ref[0, k] = jnp.sum(acc[:, k * width:(k + 1) * width]) * (1.0 / count)
 
+    state_store.wait()
     for p in range(ITERS + 1):
-        column = ag.at[p, pl.ds(0, nz - 1)]
-        rest = ag.at[p, pl.ds(0, nz * others)]
-        remote(column, column, ag_zs.at[p], ag_zr.at[p, 0], device(1, 0)).wait_send()
-        remote(rest, rest, ag_xs.at[p], ag_xr.at[p, 0], device(0, 1)).wait_send()
+        many = ag.at[p, pl.ds(0, nz * nx - 1)]
+        remote(many, many, ag_s.at[p], ag_r.at[p, 0], device(1, 0)).wait_send()
     for n in range(ITERS):
         remote(xsend.at[n], xrecv.at[n], rs_xs.at[n], rs_xr.at[n, 0], device(0, 1)).wait_send()
         remote(zsend.at[n], zrecv.at[n], rs_zs.at[n], rs_zr.at[n], device(1, 0)).wait_send()
@@ -290,13 +331,25 @@
             copy.wait_send()
 
 
+def emit(state_in, pieces_in, state_out, pieces_out, sem):
+    copies = [
+        pltpu.make_async_copy(state_in, state_out, sem.at[0]),
+        pltpu.make_async_copy(pieces_in, pieces_out, sem.at[1]),
+    ]
+    for copy in copies:
+        copy.start()
+    for copy in copies:
+        copy.wait()
+
+
 def shards(nseg, nop, psi_start, left_ops, right_ops, shifts, active):
     nx = 4 if nop == 32 else 2
     nz = nop // nx
     terms, blocks, width = left_ops.shape[1], left_ops.shape[2], left_ops.shape[3]
     vmem, dma = pltpu.VMEM, pltpu.SemaphoreType.DMA
     tile = (width, width)
-    return pl.pallas_call(
+    coded = (width + 16, width)
+    state, pieces = pl.pallas_call(
         functools.partial(kernel, nz, nx, nseg, nop),
         out_shape=(
             jax.ShapeDtypeStruct((1, 1) + tile, BF16),
@@ -306,15 +359,17 @@
             pl.BlockSpec(memory_space=pltpu.HBM),
             pl.BlockSpec(memory_space=pltpu.HBM),
             pl.BlockSpec(memory_space=pltpu.HBM),
-            pl.BlockSpec(memory_space=pltpu.SMEM),
-            pl.BlockSpec(memory_space=pltpu.SMEM),
+            pl.BlockSpec(memory_space=pltpu.HBM),
+            pl.BlockSpec(memory_space=pltpu.HBM),
         ],
         out_specs=(
-            pl.BlockSpec(memory_space=pltpu.VMEM),
+            pl.BlockSpec(memory_space=pltpu.HBM),
             pl.BlockSpec(memory_space=pltpu.SMEM),
         ),
         scratch_shapes=[
             vmem(tile, BF16),
+            pltpu.SMEM((1, terms), jnp.int32),
+            pltpu.SMEM((1, terms, blocks), jnp.int32),
             vmem((terms, blocks) + tile, BF16),
             vmem((terms, blocks) + tile, BF16),
             vmem((terms, blocks) + tile, BF16),
@@ -322,19 +377,17 @@
             vmem((ITERS, nz * (nx - 1)) + tile, BF16),
             vmem((ITERS, nz * (nx - 1)) + tile, BF16),
             vmem((nz,) + tile, F32),
-            vmem((ITERS, nz - 1) + tile, BF16),
-            vmem((ITERS, nz - 1) + tile, BF16),
+            vmem((ITERS, nz - 1) + coded, jnp.int16),
+            vmem((ITERS, nz - 1) + coded, jnp.int16),
             vmem((ITERS, nz, 8, width), F32),
             vmem((ITERS, nx, 8, width), F32),
             vmem((ITERS, 3) + tile, BF16),
             vmem(tile, F32),
             vmem(tile, F32),
             vmem(tile, F32),
-            dma((3,)),
+            dma((6,)),
             dma((ITERS + 1,)),
-            dma((ITERS + 1, nz)),
-            dma((ITERS + 1,)),
-            dma((ITERS + 1, nz)),
+            dma((ITERS + 1, nop)),
             dma((ITERS,)),
             dma((ITERS, nz)),
             dma((ITERS,)),
@@ -354,9 +407,21 @@
         psi_start,
         left_ops.reshape(left_ops.shape[1:]),
         right_ops.reshape(right_ops.shape[1:]),
-        shifts.reshape(terms),
-        active.reshape(terms, blocks),
+        shifts,
+        active,
     )
+    hbm = pl.BlockSpec(memory_space=pltpu.HBM)
+    return pl.pallas_call(
+        emit,
+        out_shape=(
+            jax.ShapeDtypeStruct(state.shape, state.dtype),
+            jax.ShapeDtypeStruct(pieces.shape, pieces.dtype),
+        ),
+        in_specs=[hbm, hbm],
+        out_specs=(hbm, hbm),
+        scratch_shapes=[dma((2,))],
+        name="emit",
+    )(state, pieces)
 
 
 def solution(mesh):

time: 129 us -> 125 us (0.969)
  local copies, waits for them, and re-layouts: 2.55 us -> 0 us
    pallas_call x1, Pallas kernels: 125 us -> 123 us  [shards(): pl.pallas_call(functools.partial(kernel, nz, nx, nseg, nop), out_shape=(j...]
    unnamed x2 -> x0, local copies, waits for them, and re-layouts: 2.55 us -> none
    pallas_call x0 -> x1, Pallas kernels: none -> 2.13 us  [shards(): pl.pallas_call(emit, out_shape=(jax.ShapeDtypeStruct(state.shape, state.d...]
where the time goes in v3:
time: 125 us
  Pallas kernels  125 us (100%)
    pallas_call x1, Pallas kernels, shards(): pl.pallas_call(functools.partial(kernel, nz, nx, nseg, nop), out_shape=(j...  123 us

profile of v3, /device:TPU:8, one launch (start us, length us, event | category | flops | bytes accessed | tf_op | source)
XLA Modules:
  0.0 125.4 jit_solution(16426360477287056962)
XLA Ops:
  0.6 122.6 %chain.1 = (bf16[1,1,128,128]{3,2,1,0:T(8,128)(2,1)}, f32[1,4]{1,0:T(1,128)}) custom-call(bf16[1,1,128,128]{3,2,1,0:T(8,128)(2,1)} %psi_hbm.1, bf16[4,32,128,128]{3,2,1,0:T(8,128)(2,1)} %bitcast.2, bf16[4,32,128,128]{3,2,1,0:T(8,128)(2,1)} %bitcast.3, s32[1,4]{1,0:T(1,128)} %shift_hbm.1, s32[1,4,32]{2,1,0:T(4,128)} %active_hbm.1), custom_call_target="tpu_custom_call" | custom-call | tf_op jit(solution)/shard_map/chain/pallas_call | solution.py:352
  123.3 2.1 %emit.1 = (bf16[1,1,128,128]{3,2,1,0:T(8,128)(2,1)}, f32[1,4]{1,0:T(1,128)}) custom-call(bf16[1,1,128,128]{3,2,1,0:T(8,128)(2,1)} %get-tuple-element.4.state_in, f32[1,4]{1,0:T(1,128)} %get-tuple-element.5.pieces_in), custom_call_target="tpu_custom_call" | custom-call | tf_op jit(solution)/shard_map/emit/pallas_call | solution.py:414

commit v4 on v3

--- a/solution.py
+++ b/solution.py
@@ -49,9 +49,9 @@
     nz, nx, nseg, axis_terms,
     psi_hbm, left_hbm, right_hbm, shift_hbm, active_hbm,
     state_hbm, rdm_ref,
-    psi_v, shift_ref, active_ref, left_v, right_v, half_v, ag, xsend, xrecv, own_acc, zsend, zrecv,
+    psi_v, shift_ref, active_ref, left_v, right_v, half_v, ag, lsend, lrecv, isend, irecv, own_acc,
     scz, scx, nbr, cur_v, tcur_v, app_v,
-    load_sem, ag_s, ag_r, rs_xs, rs_xr, rs_zs, rs_zr,
+    load_sem, ag_s, ag_r, rs_ls, rs_lr, rs_is, rs_ir,
     sc_zs, sc_zr, sc_xs, sc_xr, nb_s, nb_r,
 ):
     terms, blocks, width = left_v.shape[0], left_v.shape[1], left_v.shape[2]
@@ -160,36 +160,45 @@
         halves, rights = gathered(t)
         return lax.dot_general(halves, rights, (((1,), (1,)), ((), ())), preferred_element_type=F32)
 
-    def scatter_x(q, dz, dx):
-        place = dz * others + dx - 1
-        return remote(xsend.at[q, place], xrecv.at[q, place], rs_xs.at[q], rs_xr.at[q, dz], device(0, dx))
-
-    def scatter_z(q, dz):
-        return remote(zsend.at[q, dz - 1], zrecv.at[q, dz - 1], rs_zs.at[q], rs_zr.at[q], device(dz, 0))
+    leaves = [offset for offset in order if offset not in kids]
+    inner = [offset for offset in order if offset in kids]
+    parent_of = {child: parent for parent in kids for child in kids[parent]}
+    place = {offset: i for group in (leaves, inner) for i, offset in enumerate(group)}
+    place[(0, 0)] = len(inner)
+
+    def edge(q, offset):
+        parent, i = parent_of[offset], place[offset]
+        where = device((parent[0] - offset[0]) % nz, (parent[1] - offset[1]) % nx)
+        if offset in kids:
+            return remote(isend.at[q, i], irecv.at[q, i], rs_is.at[q], rs_ir.at[q, i], where)
+        return remote(lsend.at[q, i], lrecv.at[q, i], rs_ls.at[q], rs_lr.at[q, i], where)
 
     def scatter_send(q):
-        def row(i, carry):
-            dz = near_first(nz - 1 - i)
-            base = ((z + dz) % nz) * nx
-            parts = [term_block(base + (x + dx) % nx) for dx in range(nx)]
-            own_acc[dz] = parts[0]
-            for dx in x_order:
-                xsend[q, dz * others + dx - 1] = parts[dx].astype(BF16)
-            for dx in x_order:
-                scatter_x(q, dz, dx).start()
-            return carry
-        lax.fori_loop(0, nz, row, 0)
-
-    def column_sum(q, dz):
-        three = pl.ds(dz * others, others)
-        remote(xsend.at[q, three], xrecv.at[q, three], rs_xs.at[q], rs_xr.at[q, dz], device(0, 1)).wait_recv()
-        total = own_acc[dz]
-        for dx in range(1, nx):
-            total = total + xrecv[q, dz * others + dx - 1].astype(F32)
+        todo = leaves[::-1] + inner[::-1] + [(0, 0)]
+        for first in range(0, len(todo), 4):
+            group = todo[first:first + 4]
+            parts = [term_block(slot(*offset)) for offset in group]
+            for offset, part in zip(group, parts):
+                if offset in kids:
+                    own_acc[place[offset]] = part
+                else:
+                    lsend[q, place[offset]] = part.astype(BF16)
+            for offset in group:
+                if offset not in kids:
+                    edge(q, offset).start()
+
+    def collect(q, offset):
+        total = own_acc[place[offset]]
+        for child in sorted(kids[offset], key=order.index, reverse=True):
+            edge(q, child).wait_recv()
+            if child in kids:
+                total = total + decode(irecv.at[q, place[child]])
+            else:
+                total = total + lrecv[q, place[child]].astype(F32)
         return total
 
     def encode(ref, block):
-        largest = jnp.maximum(jnp.max(jnp.abs(block), keepdims=True), 1e-30)
+        largest = jnp.maximum(jnp.max(jnp.abs(block), axis=0, keepdims=True), 1e-30)
         exponent = jnp.ceil(jnp.log2(largest)) - 14.0
         ref[:width] = jnp.floor(block * jnp.exp2(-exponent) + 0.5).astype(jnp.int32).astype(jnp.int16)
         ref[width:] = jnp.broadcast_to(exponent, (16, width)).astype(jnp.int32).astype(jnp.int16)
@@ -198,18 +207,13 @@
         exponent = ref[width:].astype(jnp.int32).astype(F32)[0:1]
         return ref[:width].astype(jnp.int32).astype(F32) * jnp.exp2(exponent)
 
-    def scatter_finish(q):
-        def row(i, carry):
-            dz = near_first(nz - 1 - i)
-            encode(zsend.at[q, dz - 1], column_sum(q, dz))
-            scatter_z(q, dz).start()
-            return carry
-        lax.fori_loop(0, nz - 1, row, 0)
-        total = column_sum(q, 0)
-        remote(zsend.at[q], zrecv.at[q], rs_zs.at[q], rs_zr.at[q], device(1, 0)).wait_recv()
-        for dz in range(1, nz):
-            total = total + decode(zrecv.at[q, dz - 1])
-        return total * term_scale
+    def scatter_finish(q, midway):
+        for i, offset in enumerate(inner[::-1]):
+            encode(isend.at[q, place[offset]], collect(q, offset))
+            edge(q, offset).start()
+            if i == len(inner) // 2:
+                midway()
+        return collect(q, (0, 0)) * term_scale
 
     def scalars_z(q, dz):
         return remote(scz.at[q, z], scz.at[q, z], sc_zs.at[q], sc_zr.at[q], device(dz, 0))
@@ -285,8 +289,11 @@
             for copy in neighbours(n):
                 copy.start()
             tcur_v[...] = keep * tcur_v[...]
-        app_v[...] = environment(n, cur_v[...])
-        total = scatter_finish(n)
+
+        def midway(n=n):
+            app_v[...] = environment(n, cur_v[...])
+
+        total = scatter_finish(n, midway)
         if n > 0:
             total = tcur_v[...] - take * total
         applied = total + app_v[...]
@@ -321,8 +328,8 @@
         many = ag.at[p, pl.ds(0, nz * nx - 1)]
         remote(many, many, ag_s.at[p], ag_r.at[p, 0], device(1, 0)).wait_send()
     for n in range(ITERS):
-        remote(xsend.at[n], xrecv.at[n], rs_xs.at[n], rs_xr.at[n, 0], device(0, 1)).wait_send()
-        remote(zsend.at[n], zrecv.at[n], rs_zs.at[n], rs_zr.at[n], device(1, 0)).wait_send()
+        remote(lsend.at[n], lrecv.at[n], rs_ls.at[n], rs_lr.at[n, 0], device(1, 0)).wait_send()
+        remote(isend.at[n], irecv.at[n], rs_is.at[n], rs_ir.at[n, 0], device(1, 0)).wait_send()
         many = scz.at[n, pl.ds(0, nz - 1)]
         remote(many, many, sc_zs.at[n], sc_zr.at[n], device(1, 0)).wait_send()
         many = scx.at[n, pl.ds(0, others)]
@@ -349,6 +356,9 @@
     vmem, dma = pltpu.VMEM, pltpu.SemaphoreType.DMA
     tile = (width, width)
     coded = (width + 16, width)
+    order, kids = gather_tree(nz, nx)
+    n_inner = len(kids) - 1
+    n_leaf = len(order) - n_inner
     state, pieces = pl.pallas_call(
         functools.partial(kernel, nz, nx, nseg, nop),
         out_shape=(
@@ -374,11 +384,11 @@
             vmem((terms, blocks) + tile, BF16),
             vmem((terms, blocks) + tile, BF16),
             vmem((ITERS + 1, nop) + tile, BF16),
-            vmem((ITERS, nz * (nx - 1)) + tile, BF16),
-            vmem((ITERS, nz * (nx - 1)) + tile, BF16),
-            vmem((nz,) + tile, F32),
-            vmem((ITERS, nz - 1) + coded, jnp.int16),
-            vmem((ITERS, nz - 1) + coded, jnp.int16),
+            vmem((ITERS, n_leaf) + tile, BF16),
+            vmem((ITERS, n_leaf) + tile, BF16),
+            vmem((ITERS, n_inner) + coded, jnp.int16),
+            vmem((ITERS, n_inner) + coded, jnp.int16),
+            vmem((n_inner + 1,) + tile, F32),
             vmem((ITERS, nz, 8, width), F32),
             vmem((ITERS, nx, 8, width), F32),
             vmem((ITERS, 3) + tile, BF16),
@@ -389,9 +399,9 @@
             dma((ITERS + 1,)),
             dma((ITERS + 1, nop)),
             dma((ITERS,)),
-            dma((ITERS, nz)),
-            dma((ITERS,)),
-            dma((ITERS,)),
+            dma((ITERS, n_leaf)),
+            dma((ITERS,)),
+            dma((ITERS, n_inner)),
             dma((ITERS,)),
             dma((ITERS,)),
             dma((ITERS,)),

time: 125 us -> 123 us (0.984)
  Pallas kernels: 125 us -> 123 us
    pallas_call x1, Pallas kernels: 123 us -> 120 us  [shards(): pl.pallas_call(functools.partial(kernel, nz, nx, nseg, nop), out_shape=(j...]
where the time goes in v4:
time: 123 us
  Pallas kernels  123 us (100%)
    pallas_call x1, Pallas kernels, shards(): pl.pallas_call(functools.partial(kernel, nz, nx, nseg, nop), out_shape=(j...  120 us

profile of v4, /device:TPU:8, one launch (start us, length us, event | category | flops | bytes accessed | tf_op | source)
XLA Modules:
  0.0 123.4 jit_solution(3156881721176402754)
XLA Ops:
  0.6 120.5 %chain.1 = (bf16[1,1,128,128]{3,2,1,0:T(8,128)(2,1)}, f32[1,4]{1,0:T(1,128)}) custom-call(bf16[1,1,128,128]{3,2,1,0:T(8,128)(2,1)} %psi_hbm.1, bf16[4,32,128,128]{3,2,1,0:T(8,128)(2,1)} %bitcast.2, bf16[4,32,128,128]{3,2,1,0:T(8,128)(2,1)} %bitcast.3, s32[1,4]{1,0:T(1,128)} %shift_hbm.1, s32[1,4,32]{2,1,0:T(4,128)} %active_hbm.1), custom_call_target="tpu_custom_call" | custom-call | tf_op jit(solution)/shard_map/chain/pallas_call | solution.py:362
  121.1 2.1 %emit.1 = (bf16[1,1,128,128]{3,2,1,0:T(8,128)(2,1)}, f32[1,4]{1,0:T(1,128)}) custom-call(bf16[1,1,128,128]{3,2,1,0:T(8,128)(2,1)} %get-tuple-element.4.state_in, f32[1,4]{1,0:T(1,128)} %get-tuple-element.5.pieces_in), custom_call_target="tpu_custom_call" | custom-call | tf_op jit(solution)/shard_map/emit/pallas_call | solution.py:424

commit v5 on v4

--- a/solution.py
+++ b/solution.py
@@ -50,7 +50,7 @@
     psi_hbm, left_hbm, right_hbm, shift_hbm, active_hbm,
     state_hbm, rdm_ref,
     psi_v, shift_ref, active_ref, left_v, right_v, half_v, ag, lsend, lrecv, isend, irecv, own_acc,
-    scz, scx, nbr, cur_v, tcur_v, app_v,
+    scz, scx, nbr, cur_v, tcur_v, app_v, take_v,
     load_sem, ag_s, ag_r, rs_ls, rs_lr, rs_is, rs_ir,
     sc_zs, sc_zr, sc_xs, sc_xr, nb_s, nb_r,
 ):
@@ -207,12 +207,14 @@
         exponent = ref[width:].astype(jnp.int32).astype(F32)[0:1]
         return ref[:width].astype(jnp.int32).astype(F32) * jnp.exp2(exponent)
 
-    def scatter_finish(q, midway):
+    def scatter_finish(q, early, late):
         for i, offset in enumerate(inner[::-1]):
             encode(isend.at[q, place[offset]], collect(q, offset))
             edge(q, offset).start()
-            if i == len(inner) // 2:
-                midway()
+            if i == len(inner) // 5:
+                early()
+            if i == (3 * len(inner)) // 4:
+                late()
         return collect(q, (0, 0)) * term_scale
 
     def scalars_z(q, dz):
@@ -223,9 +225,9 @@
 
     def scalars_start(q, cur, applied):
         rows = lax.broadcasted_iota(jnp.int32, (8, width), 0)
-        a = jnp.sum(cur * applied)
-        b = jnp.sum(cur * cur)
-        c = jnp.sum(applied * applied)
+        a = jnp.sum(cur * applied, axis=0, keepdims=True)
+        b = jnp.sum(cur * cur, axis=0, keepdims=True)
+        c = jnp.sum(applied * applied, axis=0, keepdims=True)
         scz[q, z] = jnp.where(rows == 0, a, jnp.where(rows == 1, b, c))
         for i in range(1, nz):
             scalars_z(q, near_first(nz - i)).start()
@@ -246,6 +248,7 @@
         total = scx[q, 0]
         for xx in range(1, nx):
             total = total + scx[q, xx]
+        total = jnp.broadcast_to(jnp.sum(total, axis=1, keepdims=True), (8, width))
         a, b, c = total[0:1], total[1:2], total[2:3]
         rho = a / b
         norm = b + (STEP * STEP) * jnp.maximum(c - a * rho, 0.0)
@@ -281,21 +284,24 @@
             active_load.wait()
         gather(n, functools.partial(scalars_middle, n - 1) if n > 0 else None)
         scatter_send(n)
+
+        def update(n=n):
+            if n > 0:
+                keep, take = scalars_end(n - 1)
+                cur = keep * cur_v[...] - take * app_v[...]
+                cur_v[...] = cur
+                nbr[n, 2] = cur.astype(BF16)
+                for copy in neighbours(n):
+                    copy.start()
+                tcur_v[...] = keep * tcur_v[...]
+                take_v[...] = jnp.broadcast_to(take, take_v.shape)
+
+        def surround(n=n):
+            app_v[...] = environment(n, cur_v[...])
+
+        total = scatter_finish(n, update, surround)
         if n > 0:
-            keep, take = scalars_end(n - 1)
-            cur = keep * cur_v[...] - take * app_v[...]
-            cur_v[...] = cur
-            nbr[n, 2] = cur.astype(BF16)
-            for copy in neighbours(n):
-                copy.start()
-            tcur_v[...] = keep * tcur_v[...]
-
-        def midway(n=n):
-            app_v[...] = environment(n, cur_v[...])
-
-        total = scatter_finish(n, midway)
-        if n > 0:
-            total = tcur_v[...] - take * total
+            total = tcur_v[...] - take_v[0:1] * total
         applied = total + app_v[...]
         if n < ITERS - 1:
             ag[n + 1, me] = applied.astype(BF16)
@@ -395,6 +401,7 @@
             vmem(tile, F32),
             vmem(tile, F32),
             vmem(tile, F32),
+            vmem((8, width), F32),
             dma((6,)),
             dma((ITERS + 1,)),
             dma((ITERS + 1, nop)),

time: 123 us -> 122 us (level)
  Pallas kernels: 123 us -> 121 us
    pallas_call x1, Pallas kernels: 120 us -> 119 us  [shards(): pl.pallas_call(functools.partial(kernel, nz, nx, nseg, nop), out_shape=(j...]
where the time goes in v5:
time: 122 us
  Pallas kernels  121 us (99%)
    pallas_call x1, Pallas kernels, shards(): pl.pallas_call(functools.partial(kernel, nz, nx, nseg, nop), out_shape=(j...  119 us

profile of v5, /device:TPU:8, one launch (start us, length us, event | category | flops | bytes accessed | tf_op | source)
XLA Modules:
  0.0 121.8 jit_solution(5651678521490349627)
XLA Ops:
  0.6 118.8 %chain.1 = (bf16[1,1,128,128]{3,2,1,0:T(8,128)(2,1)}, f32[1,4]{1,0:T(1,128)}) custom-call(bf16[1,1,128,128]{3,2,1,0:T(8,128)(2,1)} %psi_hbm.1, bf16[4,32,128,128]{3,2,1,0:T(8,128)(2,1)} %bitcast.2, bf16[4,32,128,128]{3,2,1,0:T(8,128)(2,1)} %bitcast.3, s32[1,4]{1,0:T(1,128)} %shift_hbm.1, s32[1,4,32]{2,1,0:T(4,128)} %active_hbm.1), custom_call_target="tpu_custom_call" | custom-call | tf_op jit(solution)/shard_map/chain/pallas_call | solution.py:368
  119.5 2.1 %emit.1 = (bf16[1,1,128,128]{3,2,1,0:T(8,128)(2,1)}, f32[1,4]{1,0:T(1,128)}) custom-call(bf16[1,1,128,128]{3,2,1,0:T(8,128)(2,1)} %get-tuple-element.4.state_in, f32[1,4]{1,0:T(1,128)} %get-tuple-element.5.pieces_in), custom_call_target="tpu_custom_call" | custom-call | tf_op jit(solution)/shard_map/emit/pallas_call | solution.py:431
